TPU v7x, 32 devices: a whole 2x2x4 slice. The times are simulated.
32 devices in a mesh: section: 4 (over y, x), dp: 2 (over core), tensor: 4 (over z).
Axes of the slice: x: 2, y: 2, z: 4, core: 2. Of those that a mesh axis runs over, the one named last changes fastest.
Arguments:
- cotangent: bfloat16 [2, 256, 8192], P(None, 'dp', 'tensor'), may hold values from -6 to 6
- stash: bfloat16 [4, 2, 256, 8192], P('section', None, 'dp', 'tensor'), may hold values from -0.25 to 0.25
- factor_a: bfloat16 [4, 1024, 8192], P('section', 'dp', 'tensor'), may hold values from -0.0625 to 0.0625
- factor_b: bfloat16 [4, 8192, 1024], P('section', ('tensor', 'dp')), may hold values from -0.1875 to 0.1875
- block_vals: bfloat16 [4, 8, 128, 128], P('section', ('dp', 'tensor')), may hold values from -0.25 to 0.25
- block_rows: int32 [4, 8], P('section'), may hold values from 0 to 63, as said below
- block_cols: int32 [4, 8], P('section'), may hold values from 0 to 63, as said below
Outputs:
- grad_in: bfloat16 [4, 2, 256, 8192], P('section', None, 'dp', 'tensor')
- block_grad: float32 [4, 8, 128, 128], P('section', ('dp', 'tensor'))
Inputs may be any that keep to these rules, and one draw needn't show every extreme that they name: The support lies inside the diagonal part of each tensor shard. Within a section all (block_rows, block_cols) pairs are distinct. For every dp index o < 2, tensor index t < 4 and slot k < 1, the block at position (o * 4 + t) + k has both its row and its column block index in [t * 8192 // (128 * 4), (t + 1) * 8192 // (128 * 4)). `block_cols`: drawn together with block_rows; the same promise holds.
All inputs are finite; a program needn't handle non-finite values.
Results may differ from a plain program's by a relative error of at most 0.024.
Values may be sent and summed in bfloat16 or wider, within the bound.
A program may use at most 128 MiB of HBM per device.

v0:
```python
import jax
import jax.numpy as jnp
from jax import lax
from jax.sharding import PartitionSpec as P


def shifted(value, axis, steps):
    count = lax.axis_size(axis)
    initial, last = (max(0, -steps), min(count, count - steps))
    return lax.ppermute(value, axis, [(source, source + steps) for source in range(initial, last)])


def pass_back(grad_out):
    return shifted(grad_out, "section", -1)


def on_device(cotangent, stash, factor_a, factor_b, block_vals, block_rows, block_cols):
    sections = lax.axis_size("section")
    section_pos = lax.axis_index("section")
    tensor_pos = lax.axis_index("tensor")
    dp_count = lax.axis_size("dp")
    tensor_count = lax.axis_size("tensor")
    left_full, right_full, values = (
        lax.all_gather(factor_a[0], "dp", axis=0, tiled=True),
        lax.all_gather(factor_b[0], "dp", axis=0, tiled=True),
        lax.all_gather(block_vals[0], "dp", axis=0, tiled=True),
    )
    batches = stash.shape[1]
    tokens_here = stash.shape[2]
    local_width = stash.shape[3]
    block_size = block_vals.shape[-1]
    local_blocks = local_width // block_size

    def local_ids(table):
        grid = table[0].reshape(dp_count, tensor_count, -1)
        mine = lax.dynamic_index_in_dim(grid, tensor_pos, 1, keepdims=False)
        return mine.reshape(-1) - tensor_pos * local_blocks

    positions = jnp.arange(local_blocks, dtype=jnp.int32)[None, :]
    row_hits = local_ids(block_rows)[:, None] == positions
    col_hits = local_ids(block_cols)[:, None] == positions
    row_pick = row_hits.astype(jnp.bfloat16)
    row_double = jnp.concatenate([row_pick, row_pick], axis=0)
    col_pick = col_hits.astype(jnp.bfloat16)
    grad_sum = jnp.zeros((values.shape[0], block_size, block_size), jnp.float32)
    grads_in = jnp.zeros(stash.shape[1:], jnp.bfloat16)
    received = jnp.zeros((tokens_here, local_width), jnp.bfloat16)
    steps = batches + sections - 1
    for step_idx in range(steps):
        batch_pos = step_idx - (sections - 1 - section_pos)
        active = (batch_pos >= 0) & (batch_pos < batches)
        slot_pos = jnp.clip(batch_pos, 0, batches - 1)
        fresh = lax.dynamic_index_in_dim(cotangent, slot_pos, 0, keepdims=False)
        cot_now = jnp.where(section_pos == sections - 1, fresh, received)
        partial_value = jnp.einsum(
            "td,rd->tr", cot_now, left_full, preferred_element_type=jnp.float32
        )
        share = lax.psum_scatter(
            partial_value.astype(jnp.bfloat16), "tensor", scatter_dimension=1, tiled=True
        )
        rank_act = lax.all_gather(share, "tensor", axis=1, tiled=True)
        picked_cot = jnp.einsum(
            "tlc,nl->tnc",
            cot_now.reshape(tokens_here, local_blocks, block_size),
            col_pick,
            preferred_element_type=jnp.float32,
        ).astype(jnp.bfloat16)
        sparse_terms = jnp.einsum(
            "tnc,nrc->tnr", picked_cot, values, preferred_element_type=jnp.float32
        )
        upper_part = sparse_terms.astype(jnp.bfloat16)
        lower_part = (sparse_terms - upper_part.astype(jnp.float32)).astype(jnp.bfloat16)
        both_parts = jnp.concatenate([upper_part, lower_part], axis=1)
        sparse_grad = jnp.einsum(
            "tnr,nl->tlr", both_parts, row_double, preferred_element_type=jnp.float32
        )
        dense_grad = jnp.einsum(
            "tr,dr->td", rank_act, right_full, preferred_element_type=jnp.float32
        )
        grad_out = (dense_grad + sparse_grad.reshape(tokens_here, local_width)).astype(jnp.bfloat16)
        current = lax.dynamic_index_in_dim(grads_in, slot_pos, 0, keepdims=False)
        grads_in = lax.dynamic_update_index_in_dim(
            grads_in, jnp.where(active, grad_out, current), slot_pos, 0
        )
        stash_now = lax.dynamic_index_in_dim(stash[0], slot_pos, 0, keepdims=False)
        live_scale = active.astype(jnp.bfloat16)
        if step_idx + 1 < steps:
            received = pass_back(grad_out)
        picked_in = (
            jnp.einsum(
                "tlr,nl->tnr",
                stash_now.reshape(tokens_here, local_blocks, block_size),
                row_pick,
                preferred_element_type=jnp.float32,
            ).astype(jnp.bfloat16)
            * live_scale
        )
        grad_sum = grad_sum + jnp.einsum(
            "tnr,tnc->nrc", picked_in, picked_cot, preferred_element_type=jnp.float32
        )
    block_grad = lax.psum_scatter(
        grad_sum.astype(jnp.bfloat16), "dp", scatter_dimension=0, tiled=True
    ).astype(jnp.float32)
    return (grads_in[None], block_grad[None])


def solution(mesh):
    in_specs = (
        P(None, "dp", "tensor"),
        P("section", None, "dp", "tensor"),
        P("section", "dp", "tensor"),
        P("section", ("tensor", "dp"), None),
        P("section", ("dp", "tensor"), None, None),
        P("section", None),
        P("section", None),
    )
    out_specs = (P("section", None, "dp", "tensor"), P("section", ("dp", "tensor"), None, None))
    return jax.shard_map(
        on_device, mesh=mesh, in_specs=in_specs, out_specs=out_specs, check_vma=False
    )
```

profile of v0, /device:TPU:0, one launch (start us, length us, event | category | flops | bytes accessed | tf_op | source)
XLA Modules:
  0.0 300.2 jit_solution(10202126768568250833)
XLA Ops:
  7.2 0.7 all-gather.6.cloned.1.call-update
  8.0 17.9 %all-gather.6.cloned.1.call-done = bf16[1,1024,2048]{2,1,0:T(8,128)(2,1)} async-done(((bf16[1,512,2048]{2,1,0:T(8,128)(2,1)}), bf16[1,1024,2048]{2,1,0:T(8,128)(2,1)}) %all-gather.6.cloned.1.call-update) | async-done | bytes 4194320 | tf_op jit(solution)/shard_map/all_gather | solution.py:24
  25.9 4.6 %fusion.59 = bf16[128,1024]{1,0:T(8,128)(2,1)} fusion(bf16[1,1024,2048]{2,1,0:T(8,128)(2,1)} %all-gather.6.cloned.1.call-done, bf16[2,128,2048]{2,1,0:T(8,128)(2,1)} %param.7, s32[]{:T(128)S(6)} %min.16, pred[]{:T(512)S(6)} %eq.14), kind=kOutput, calls=%fused_computation.33 | convolution fusion | flops 537264128 | bytes 4980741 | tf_op jit(solution)/shard_map/td,rd->tr/dot_general | solution.py:55
  30.6 0.7 all-gather.8.cloned.1.call-update
  31.5 0.5 broadcast.42
  32.0 0.7 reduce.11
  32.8 0.7 reduce.10
  33.6 1.5 dynamic-slice_bitcast_fusion
  35.0 0.9 copy.71
  36.2 1.9 all-gather.2
  38.0 0.3 fusion.75
  38.6 0.4 fusion.105
  39.0 12.9 %reduce-scatter.7.cloned.1.call-done = bf16[128,256]{1,0:T(8,128)(2,1)} async-done(((bf16[128,1024]{1,0:T(8,128)(2,1)}), bf16[128,256]{1,0:T(8,128)(2,1)}) %reduce-scatter.7.cloned.1.call-update) | async-done | bytes 65552 | tf_op jit(solution)/shard_map/reduce_scatter | solution.py:58
  51.9 14.0 %all_gather.25 = bf16[128,1024]{1,0:T(8,128)(2,1)S(1)} all-gather(bf16[128,256]{1,0:T(8,128)(2,1)} %reduce-scatter.7.cloned.1.call-done), channel_id=1, replica_groups=mesh['section'=4,'dp'=2,'tensor'=4] {'tensor'}, dimensions={1}, use_global_device_ids=true | all-gather | bytes 327680 | tf_op jit(solution)/shard_map/all_gather | solution.py:61
  66.0 4.7 %bitcast_dynamic-update-slice_fusion.3 = (bf16[2,128,2048]{2,1,0:T(8,128)(2,1)S(1)}, bf16[128,2048]{1,0:T(8,128)(2,1)}) fusion(bf16[2,128,2048]{2,1,0:T(8,128)(2,1)S(1)} %broadcast_in_dim.36, s32[]{:T(128)S(6)} %min.16, pred[]{:T(512)S(6)} %and.17, f32[16,8,16,128]{3,2,1,0:T(8,128)S(1)} %bitcast.277, bf16[128,1024]{1,0:T(8,128)(2,1)S(1)} %all_gather.25, ...), kind=kOutput, calls=%fused_computation.83 | convolution fusion | flops 537657344 | bytes 6553605 | tf_op jit(solution)/shard_map/tr,dr->td/dot_general | solution.py:77
  70.7 1.3 collective-permute-start
  72.0 2.0 fusion.81
  74.0 1.1 copy.72
  75.1 2.0 copy.73
  77.1 0.9 fusion.83
  78.0 0.8 constant_dynamic-slice_fusion.2
  78.8 7.5 %collective-permute-done = bf16[128,2048]{1,0:T(8,128)(2,1)S(1)} collective-permute-done((bf16[128,2048]{1,0:T(8,128)(2,1)}, bf16[128,2048]{1,0:T(8,128)(2,1)S(1)}, u32[]{:S(2)}, u32[]{:S(2)}) %collective-permute-start) | collective-permute-done | bytes 524320 | tf_op jit(solution)/shard_map/ppermute | solution.py:10
  86.6 0.3 fusion.76
  86.8 2.2 fusion.62
  89.4 0.4 fusion.103
  89.8 20.7 %reduce-scatter.9.cloned.1.call-done = bf16[128,256]{1,0:T(8,128)(2,1)} async-done(((bf16[128,1024]{1,0:T(8,128)(2,1)}), bf16[128,256]{1,0:T(8,128)(2,1)}) %reduce-scatter.9.cloned.1.call-update) | async-done | bytes 65552 | tf_op jit(solution)/shard_map/reduce_scatter | solution.py:58
  110.4 14.2 %all_gather.28 = bf16[128,1024]{1,0:T(8,128)(2,1)S(1)} all-gather(bf16[128,256]{1,0:T(8,128)(2,1)} %reduce-scatter.9.cloned.1.call-done), channel_id=1, replica_groups=mesh['section'=4,'dp'=2,'tensor'=4] {'tensor'}, dimensions={1}, use_global_device_ids=true | all-gather | bytes 327680 | tf_op jit(solution)/shard_map/all_gather | solution.py:61
  124.6 4.8 %bitcast_dynamic-update-slice_fusion.2 = (bf16[2,128,2048]{2,1,0:T(8,128)(2,1)S(1)}, bf16[128,2048]{1,0:T(8,128)(2,1)}) fusion(bf16[2,128,2048]{2,1,0:T(8,128)(2,1)S(1)} %get-tuple-element.17, s32[]{:T(128)S(6)} %min.17, bf16[1,128,2048]{2,1,0:T(8,128)(2,1)} %constant_dynamic-slice_fusion.2, pred[]{:T(512)S(6)} %and.18, ...), kind=kOutput, calls=%fused_computation.80 | convolution fusion | flops 537657344 | bytes 7077893 | tf_op jit(solution)/shard_map/tr,dr->td/dot_general | solution.py:77
  129.4 1.3 collective-permute-start.1
  130.7 0.9 fusion.85
  131.6 1.1 copy.74
  132.8 0.9 fusion.87
  133.7 0.8 constant_dynamic-slice_fusion.1
  134.6 6.4 %collective-permute-done.1 = bf16[128,2048]{1,0:T(8,128)(2,1)S(1)} collective-permute-done((bf16[128,2048]{1,0:T(8,128)(2,1)}, bf16[128,2048]{1,0:T(8,128)(2,1)S(1)}, u32[]{:S(2)}, u32[]{:S(2)}) %collective-permute-start.1) | collective-permute-done | bytes 524320 | tf_op jit(solution)/shard_map/ppermute | solution.py:10
  141.2 0.3 fusion.77
  141.4 2.2 fusion.65
  144.0 0.4 fusion.101
  144.4 17.8 %reduce-scatter.11.cloned.1.call-done = bf16[128,256]{1,0:T(8,128)(2,1)} async-done(((bf16[128,1024]{1,0:T(8,128)(2,1)}), bf16[128,256]{1,0:T(8,128)(2,1)}) %reduce-scatter.11.cloned.1.call-update) | async-done | bytes 65552 | tf_op jit(solution)/shard_map/reduce_scatter | solution.py:58
  162.2 14.4 %all_gather.29 = bf16[128,1024]{1,0:T(8,128)(2,1)S(1)} all-gather(bf16[128,256]{1,0:T(8,128)(2,1)} %reduce-scatter.11.cloned.1.call-done), channel_id=1, replica_groups=mesh['section'=4,'dp'=2,'tensor'=4] {'tensor'}, dimensions={1}, use_global_device_ids=true | all-gather | bytes 327680 | tf_op jit(solution)/shard_map/all_gather | solution.py:61
  176.6 4.8 %bitcast_dynamic-update-slice_fusion.1 = (bf16[2,128,2048]{2,1,0:T(8,128)(2,1)S(1)}, bf16[128,2048]{1,0:T(8,128)(2,1)}) fusion(bf16[2,128,2048]{2,1,0:T(8,128)(2,1)S(1)} %get-tuple-element.19, s32[]{:T(128)S(6)} %min.18, bf16[1,128,2048]{2,1,0:T(8,128)(2,1)} %constant_dynamic-slice_fusion.1, pred[]{:T(512)S(6)} %and.19, ...), kind=kOutput, calls=%fused_computation.77 | convolution fusion | flops 537657344 | bytes 7077893 | tf_op jit(solution)/shard_map/tr,dr->td/dot_general | solution.py:77
  181.4 1.3 collective-permute-start.2
  182.7 0.9 fusion.116
  183.6 1.1 copy.75
  184.7 0.9 fusion.89
  185.6 0.9 constant_dynamic-slice_fusion
  186.6 6.2 %collective-permute-done.2 = bf16[128,2048]{1,0:T(8,128)(2,1)S(1)} collective-permute-done((bf16[128,2048]{1,0:T(8,128)(2,1)}, bf16[128,2048]{1,0:T(8,128)(2,1)S(1)}, u32[]{:S(2)}, u32[]{:S(2)}) %collective-permute-start.2) | collective-permute-done | bytes 524320 | tf_op jit(solution)/shard_map/ppermute | solution.py:10
  192.9 0.3 fusion.78
  193.2 2.2 fusion.68
  195.8 0.4 fusion.99
  196.2 17.9 %reduce-scatter.13.cloned.1.call-done = bf16[128,256]{1,0:T(8,128)(2,1)} async-done(((bf16[128,1024]{1,0:T(8,128)(2,1)}), bf16[128,256]{1,0:T(8,128)(2,1)}) %reduce-scatter.13.cloned.1.call-update) | async-done | bytes 65552 | tf_op jit(solution)/shard_map/reduce_scatter | solution.py:58
  214.0 14.2 %all_gather.30 = bf16[128,1024]{1,0:T(8,128)(2,1)S(1)} all-gather(bf16[128,256]{1,0:T(8,128)(2,1)} %reduce-scatter.13.cloned.1.call-done), channel_id=1, replica_groups=mesh['section'=4,'dp'=2,'tensor'=4] {'tensor'}, dimensions={1}, use_global_device_ids=true | all-gather | bytes 327680 | tf_op jit(solution)/shard_map/all_gather | solution.py:61
  228.2 4.0 %bitcast_dynamic-update-slice_fusion = (bf16[2,128,2048]{2,1,0:T(8,128)(2,1)S(1)}, bf16[128,2048]{1,0:T(8,128)(2,1)S(1)}) fusion(bf16[2,128,2048]{2,1,0:T(8,128)(2,1)S(1)} %get-tuple-element.21, s32[]{:T(128)S(6)} %min.19, bf16[1,128,2048]{2,1,0:T(8,128)(2,1)} %constant_dynamic-slice_fusion, pred[]{:T(512)S(6)} %and.20, ...), kind=kOutput, calls=%fused_computation.74 | convolution fusion | flops 537657344 | bytes 7077893 | tf_op jit(solution)/shard_map/tr,dr->td/dot_general | solution.py:77
  232.3 1.4 collective-permute-start.3
  234.4 1.0 copy.135
  235.3 8.4 %collective-permute-done.3 = bf16[128,2048]{1,0:T(8,128)(2,1)S(1)} collective-permute-done((bf16[128,2048]{1,0:T(8,128)(2,1)S(1)}, bf16[128,2048]{1,0:T(8,128)(2,1)S(1)}, u32[]{:S(2)}, u32[]{:S(2)}) %collective-permute-start.3) | collective-permute-done | bytes 524320 | tf_op jit(solution)/shard_map/ppermute | solution.py:10
  243.9 0.3 fusion.79
  244.2 0.9 fusion.74
  245.1 4.4 %fusion.71 = bf16[128,1024]{1,0:T(8,128)(2,1)} fusion(bf16[1,1024,2048]{2,1,0:T(8,128)(2,1)} %all-gather.6.cloned.1.call-done, bf16[128,2048]{1,0:T(8,128)(2,1)S(1)} %collective-permute-done.3, bf16[2,128,2048]{2,1,0:T(8,128)(2,1)S(1)} %copy-done.3, s32[]{:T(128)S(6)} %min.20, pred[]{:T(512)S(6)} %eq.14), kind=kOutput, calls=%fused_computation.37 | convolution fusion | flops 537264128 | bytes 5505029 | tf_op jit(solution)/shard_map/td,rd->tr/dot_general | solution.py:55
  249.8 0.4 fusion.97
  250.2 1.0 reduce-scatter.17.cloned.1.call-done
  251.2 1.4 bitcast_convert_fusion
  252.5 22.0 %reduce-scatter.15.cloned.1.call-done = bf16[128,256]{1,0:T(8,128)(2,1)} async-done(((bf16[128,1024]{1,0:T(8,128)(2,1)}), bf16[128,256]{1,0:T(8,128)(2,1)}) %reduce-scatter.15.cloned.1.call-update) | async-done | bytes 65552 | tf_op jit(solution)/shard_map/reduce_scatter | solution.py:58
  274.5 14.2 %all_gather.31 = bf16[128,1024]{1,0:T(8,128)(2,1)S(1)} all-gather(bf16[128,256]{1,0:T(8,128)(2,1)} %reduce-scatter.15.cloned.1.call-done), channel_id=1, replica_groups=mesh['section'=4,'dp'=2,'tensor'=4] {'tensor'}, dimensions={1}, use_global_device_ids=true | all-gather | bytes 327680 | tf_op jit(solution)/shard_map/all_gather | solution.py:61
  288.7 4.7 %fusion.56 = bf16[1,2,128,2048]{3,2,1,0:T(8,128)(2,1)} fusion(bf16[1,2,128,2048]{3,2,1,0:T(8,128)(2,1)} %copy.135, s32[]{:T(128)S(6)} %min.20, bf16[128,1024]{1,0:T(8,128)(2,1)S(1)} %all_gather.31, bf16[1,2048,1024]{2,1,0:T(8,128)(2,1)} %all-gather.8.cloned.1.call-done, f32[16,8,16,128]{3,2,1,0:T(8,128)S(1)} %bitcast.276, ...), kind=kOutput, calls=%fused_computation.32 | convolution fusion | flops 537657344 | bytes 6553605 | tf_op jit(solution)/shard_map/tr,dr->td/dot_general | solution.py:77
  (73 shorter events, 3.5 us)
Async XLA Ops:
  7.2 18.8 %all-gather.6.cloned.1.call-start = ((), (), s32[]{:S(2)}) async-start(), calls=%async_computation.12 | async-start | bytes 6291456 | tf_op jit(solution)/shard_map/all_gather | solution.py:24
  7.9 23.4 %copy-start.3 = (bf16[2,128,2048]{2,1,0:T(8,128)(2,1)S(1)}, bf16[2,128,2048]{2,1,0:T(8,128)(2,1)}, u32[]{:S(2)}) copy-start(bf16[2,128,2048]{2,1,0:T(8,128)(2,1)} %param.7) | copy-start | bytes 3145732
  7.9 44.0 %reduce-scatter.7.cloned.1.call-start = ((), (), s32[]{:S(2)}) async-start(), calls=%async_computation.6 | async-start | bytes 327680 | tf_op jit(solution)/shard_map/reduce_scatter | solution.py:58
  8.0 24.1 %copy-start.13 = (s32[1,8]{1,0:T(1,128)S(1)}, s32[1,8]{1,0:T(1,128)}, u32[]{:S(2)}) copy-start(s32[1,8]{1,0:T(1,128)} %param.12) | copy-start | bytes 100
  8.0 24.8 %copy-start.14 = (s32[1,8]{1,0:T(1,128)S(1)}, s32[1,8]{1,0:T(1,128)}, u32[]{:S(2)}) copy-start(s32[1,8]{1,0:T(1,128)} %param.13) | copy-start | bytes 100
  8.0 25.6 %copy-start.4 = (bf16[1,2,128,2048]{3,2,1,0:T(8,128)(2,1)S(1)}, bf16[1,2,128,2048]{3,2,1,0:T(8,128)(2,1)}, u32[]{:S(2)}) copy-start(bf16[1,2,128,2048]{3,2,1,0:T(8,128)(2,1)} %param.8) | copy-start | bytes 3145732
  30.5 35.3 %all-gather.8.cloned.1.call-start = ((), (), s32[]{:S(2)}) async-start(), calls=%async_computation.13 | async-start | bytes 6291456 | tf_op jit(solution)/shard_map/all_gather | solution.py:25
  31.3 79.2 %reduce-scatter.9.cloned.1.call-start = ((), (), s32[]{:S(2)}) async-start(), calls=%async_computation.7 | async-start | bytes 327680 | tf_op jit(solution)/shard_map/reduce_scatter | solution.py:58
  31.3 4.8 %copy-start.12 = (bf16[1,1,128,128]{3,2,1,0:T(8,128)(2,1)S(1)}, bf16[1,1,128,128]{3,2,1,0:T(8,128)(2,1)}, u32[]{:S(2)}) copy-start(bf16[1,1,128,128]{3,2,1,0:T(8,128)(2,1)} %param.11) | copy-start | bytes 98308
  70.7 15.7 %collective-permute-start = (bf16[128,2048]{1,0:T(8,128)(2,1)}, bf16[128,2048]{1,0:T(8,128)(2,1)S(1)}, u32[]{:S(2)}, u32[]{:S(2)}) collective-permute-start(bf16[128,2048]{1,0:T(8,128)(2,1)} %get-tuple-element.18), channel_id=1, source_target_pairs={{8,0},{16,8},{24,16},{9,1},{17,9},{25,17},{10,2},{18,10},{26,18},{... | collective-permute-start | bytes 1572872 | tf_op jit(solution)/shard_map/ppermute | solution.py:10
  77.1 9.7 %copy-start = (bf16[1,1024,2048]{2,1,0:T(8,128)(2,1)S(1)}, bf16[1,1024,2048]{2,1,0:T(8,128)(2,1)}, u32[]{:S(2)}) copy-start(bf16[1,1024,2048]{2,1,0:T(8,128)(2,1)} %all-gather.6.cloned.1.call-done) | copy-start | bytes 12582916
  89.1 73.1 %reduce-scatter.11.cloned.1.call-start = ((), (), s32[]{:S(2)}) async-start(), calls=%async_computation.8 | async-start | bytes 327680 | tf_op jit(solution)/shard_map/reduce_scatter | solution.py:58
  110.4 20.3 %copy-start.5 = (bf16[16,8,16,128]{3,2,1,0:T(8,128)(2,1)S(1)}, bf16[16,8,16,128]{3,2,1,0:T(8,128)(2,1)}, u32[]{:S(2)}) copy-start(bf16[16,8,16,128]{3,2,1,0:T(8,128)(2,1)} %copy.73) | copy-start | bytes 1572868
  129.4 11.6 %collective-permute-start.1 = (bf16[128,2048]{1,0:T(8,128)(2,1)}, bf16[128,2048]{1,0:T(8,128)(2,1)S(1)}, u32[]{:S(2)}, u32[]{:S(2)}) collective-permute-start(bf16[128,2048]{1,0:T(8,128)(2,1)} %get-tuple-element.20), channel_id=1, source_target_pairs={{8,0},{16,8},{24,16},{9,1},{17,9},{25,17},{10,2},{18,10},{26,18},{... | collective-permute-start | bytes 1572872 | tf_op jit(solution)/shard_map/ppermute | solution.py:10
  132.8 8.7 %copy-start.1 = (bf16[1,1024,2048]{2,1,0:T(8,128)(2,1)S(1)}, bf16[1,1024,2048]{2,1,0:T(8,128)(2,1)}, u32[]{:S(2)}) copy-start(bf16[1,1024,2048]{2,1,0:T(8,128)(2,1)} %all-gather.6.cloned.1.call-done) | copy-start | bytes 12582916
  143.7 70.3 %reduce-scatter.13.cloned.1.call-start = ((), (), s32[]{:S(2)}) async-start(), calls=%async_computation.9 | async-start | bytes 327680 | tf_op jit(solution)/shard_map/reduce_scatter | solution.py:58
  144.4 38.3 %copy-start.9 = (bf16[128,2,128]{2,1,0:T(2,128)(2,1)S(1)}, bf16[128,2,128]{2,1,0:T(2,128)(2,1)}, u32[]{:S(2)}) copy-start(bf16[128,2,128]{2,1,0:T(2,128)(2,1)} %fusion.81) | copy-start | bytes 196612
  181.4 11.4 %collective-permute-start.2 = (bf16[128,2048]{1,0:T(8,128)(2,1)}, bf16[128,2048]{1,0:T(8,128)(2,1)S(1)}, u32[]{:S(2)}, u32[]{:S(2)}) collective-permute-start(bf16[128,2048]{1,0:T(8,128)(2,1)} %get-tuple-element.22), channel_id=1, source_target_pairs={{8,0},{16,8},{24,16},{9,1},{17,9},{25,17},{10,2},{18,10},{26,18},{... | collective-permute-start | bytes 1572872 | tf_op jit(solution)/shard_map/ppermute | solution.py:10
  184.7 8.5 %copy-start.2 = (bf16[1,1024,2048]{2,1,0:T(8,128)(2,1)S(1)}, bf16[1,1024,2048]{2,1,0:T(8,128)(2,1)}, u32[]{:S(2)}) copy-start(bf16[1,1024,2048]{2,1,0:T(8,128)(2,1)} %all-gather.6.cloned.1.call-done) | copy-start | bytes 12582916
  195.5 55.6 %reduce-scatter.17.cloned.1.call-start = ((), (), s32[]{:S(2)}) async-start(), calls=%async_computation.11 | async-start | bytes 98304 | tf_op jit(solution)/shard_map/reduce_scatter | solution.py:101
  195.8 37.9 %copy-start.6 = (f32[2,128,128]{2,1,0:T(8,128)S(1)}, f32[2,128,128]{2,1,0:T(8,128)}, u32[]{:S(2)}) copy-start(f32[2,128,128]{2,1,0:T(8,128)} %fusion.116) | copy-start | bytes 393220
  214.0 19.7 %copy-start.8 = (bf16[128,2,128]{2,1,0:T(2,128)(2,1)S(1)}, bf16[128,2,128]{2,1,0:T(2,128)(2,1)}, u32[]{:S(2)}) copy-start(bf16[128,2,128]{2,1,0:T(2,128)(2,1)} %fusion.83) | copy-start | bytes 196612
  214.0 19.9 %copy-start.10 = (bf16[128,2,128]{2,1,0:T(2,128)(2,1)S(1)}, bf16[128,2,128]{2,1,0:T(2,128)(2,1)}, u32[]{:S(2)}) copy-start(bf16[128,2,128]{2,1,0:T(2,128)(2,1)} %fusion.85) | copy-start | bytes 196612
  214.0 20.1 %copy-start.11 = (bf16[128,2,128]{2,1,0:T(2,128)(2,1)S(1)}, bf16[128,2,128]{2,1,0:T(2,128)(2,1)}, u32[]{:S(2)}) copy-start(bf16[128,2,128]{2,1,0:T(2,128)(2,1)} %fusion.87) | copy-start | bytes 196612
  232.2 12.0 %copy-start.7 = (bf16[128,2,128]{2,1,0:T(2,128)(2,1)S(1)}, bf16[128,2,128]{2,1,0:T(2,128)(2,1)}, u32[]{:S(2)}) copy-start(bf16[128,2,128]{2,1,0:T(2,128)(2,1)} %fusion.89) | copy-start | bytes 196612
  232.3 11.5 %collective-permute-start.3 = (bf16[128,2048]{1,0:T(8,128)(2,1)S(1)}, bf16[128,2048]{1,0:T(8,128)(2,1)S(1)}, u32[]{:S(2)}, u32[]{:S(2)}) collective-permute-start(bf16[128,2048]{1,0:T(8,128)(2,1)S(1)} %get-tuple-element.24), channel_id=1, source_target_pairs={{8,0},{16,8},{24,16},{9,1},{17,9},{25,17},{10,2},{18,10},{26,18},{... | collective-permute-start | bytes 1572872 | tf_op jit(solution)/shard_map/ppermute | solution.py:10
  245.1 29.4 %reduce-scatter.15.cloned.1.call-start = ((), (), s32[]{:S(2)}) async-start(), calls=%async_computation.10 | async-start | bytes 327680 | tf_op jit(solution)/shard_map/reduce_scatter | solution.py:58
Sparse Core Ops, SparseCore 0:
  9.5 16.3 all-gather.5
  30.7 21.1 reduce-scatter.6
  53.4 11.8 all-gather.7
  89.2 21.1 reduce-scatter.8
  143.8 18.3 reduce-scatter.10
  195.6 18.3 reduce-scatter.12
  245.2 5.9 reduce-scatter.16
  253.4 21.0 reduce-scatter.14
where the time goes:
time: 301 us; the launch traced here: 300 us
  waiting for transfers between devices  140 us (47%)
  blocking collectives  72.7 us (24%)
  matrix products  51 us (17%)
  between operations  14.6 us (5%)
  local copies, waits for them, and re-layouts  12.8 us (4%)
  starting transfers between devices  5.59 us (2%)
  other arithmetic  3.35 us (1%)
    reduce_scatter x5, waiting for transfers between devices, on_device(): lax.psum_scatter(partial_value.astype(jnp.bfloat16), 'tensor', scatter_di...  91.2 us
    all_gather x5, blocking collectives, on_device(): rank_act = lax.all_gather(share, 'tensor', axis=1, tiled=True)  70.8 us
    ppermute x4, waiting for transfers between devices, shifted(): lax.ppermute(value, axis, [(source, source + steps) for source in range(i...  28.5 us
    dot_general x5, matrix products, on_device(): jnp.einsum('tr,dr->td', rank_act, right_full, preferred_element_type=jnp....  23.1 us
    all_gather x1, waiting for transfers between devices, on_device(): lax.all_gather(factor_a[0], 'dp', axis=0, tiled=True)  17.9 us
    dot_general x5, matrix products, on_device(): jnp.einsum('td,rd->tr', cot_now, left_full, preferred_element_type=jnp.fl...  15.7 us
    unnamed x43, local copies, waits for them, and re-layouts  9.95 us
  transfers between devices with their start and end apart: 12, of which 11 were waited for; matrix products, arithmetic and copies ran while one was open for 10% of the time, Pallas kernels for 0%

commit v1 on v0

--- a/solution.py
+++ b/solution.py
@@ -58,7 +58,16 @@
         share = lax.psum_scatter(
             partial_value.astype(jnp.bfloat16), "tensor", scatter_dimension=1, tiled=True
         )
-        rank_act = lax.all_gather(share, "tensor", axis=1, tiled=True)
+        ring = [share]
+        for hop in range(3):
+            ring.append(
+                lax.ppermute(ring[-1], "tensor", [(dev, (dev + 1) % 4) for dev in range(4)])
+            )
+        rank_act = jnp.roll(
+            jnp.concatenate(ring[::-1], axis=1),
+            (lax.axis_index("tensor") + 1) * ring[0].shape[1],
+            axis=1,
+        )
         picked_cot = jnp.einsum(
             "tlc,nl->tnc",
             cot_now.reshape(tokens_here, local_blocks, block_size),

time: 301 us -> 315 us (1.047)
  waiting for transfers between devices: 140 us -> 220 us
  blocking collectives: 72.7 us -> 1.85 us
  matrix products: 51 us -> 57.5 us
  local copies, waits for them, and re-layouts: 12.8 us -> 8.54 us
  other arithmetic: 3.35 us -> 6.5 us
    ppermute x0 -> x15, waiting for transfers between devices: none -> 89.2 us  [on_device(): lax.ppermute(ring[-1], 'tensor', [(dev, (dev + 1) % 4) for dev in range(4)])]
    all_gather x5 -> x0, blocking collectives: 70.8 us -> none  [on_device(): rank_act = lax.all_gather(share, 'tensor', axis=1, tiled=True)]
    reduce_scatter x5, waiting for transfers between devices: 91.2 us -> 83.9 us  [on_device(): lax.psum_scatter(partial_value.astype(jnp.bfloat16), 'tensor', scatter_di...]
    dot_general x5, matrix products: 15.7 us -> 20.5 us  [on_device(): jnp.einsum('td,rd->tr', cot_now, left_full, preferred_element_type=jnp.fl...]
    unnamed x43, local copies, waits for them, and re-layouts: 9.95 us -> 6.54 us
  transfers between devices with their start and end apart: 12 -> 27, of which waited for: 11 -> 25; matrix products, arithmetic and copies ran while one was open for 10% -> 9% of each run, Pallas kernels for 0% -> 0%
where the time goes in v1:
time: 315 us
  waiting for transfers between devices  220 us (70%)
  matrix products  57.5 us (18%)
  between operations  14.6 us (5%)
  local copies, waits for them, and re-layouts  8.54 us (3%)
  other arithmetic  6.5 us (2%)
  starting transfers between devices  5.76 us (2%)
    ppermute x15, waiting for transfers between devices, on_device(): lax.ppermute(ring[-1], 'tensor', [(dev, (dev + 1) % 4) for dev in range(4)])  89.2 us
    reduce_scatter x5, waiting for transfers between devices, on_device(): lax.psum_scatter(partial_value.astype(jnp.bfloat16), 'tensor', scatter_di...  83.9 us
    ppermute x4, waiting for transfers between devices, shifted(): lax.ppermute(value, axis, [(source, source + steps) for source in range(i...  27.6 us
    dot_general x5, matrix products, on_device(): jnp.einsum('tr,dr->td', rank_act, right_full, preferred_element_type=jnp....  24 us
    dot_general x5, matrix products, on_device(): jnp.einsum('td,rd->tr', cot_now, left_full, preferred_element_type=jnp.fl...  20.5 us
    all_gather x1, waiting for transfers between devices, on_device(): lax.all_gather(factor_a[0], 'dp', axis=0, tiled=True)  17.9 us
    unnamed x43, local copies, waits for them, and re-layouts  6.54 us
  transfers between devices with their start and end apart: 27, of which 25 were waited for; matrix products, arithmetic and copies ran while one was open for 9% of the time, Pallas kernels for 0%

profile of v1, /device:TPU:0, one launch (start us, length us, event | category | flops | bytes accessed | tf_op | source)
XLA Modules:
  0.0 314.9 jit_solution(6753509634754021329)
XLA Ops:
  7.2 0.7 all-gather.6.cloned.1.call-update
  8.0 17.9 %all-gather.6.cloned.1.call-done = bf16[1,1024,2048]{2,1,0:T(8,128)(2,1)} async-done(((bf16[1,512,2048]{2,1,0:T(8,128)(2,1)}), bf16[1,1024,2048]{2,1,0:T(8,128)(2,1)}) %all-gather.6.cloned.1.call-update) | async-done | bytes 4194320 | tf_op jit(solution)/shard_map/all_gather | solution.py:24
  25.9 4.6 %fusion.59 = bf16[128,1024]{1,0:T(8,128)(2,1)} fusion(bf16[1,1024,2048]{2,1,0:T(8,128)(2,1)} %all-gather.6.cloned.1.call-done, bf16[2,128,2048]{2,1,0:T(8,128)(2,1)} %param.9, s32[]{:T(128)S(6)} %min.16, pred[]{:T(512)S(6)} %eq.15), kind=kOutput, calls=%fused_computation.33 | convolution fusion | flops 537264128 | bytes 4980741 | tf_op jit(solution)/shard_map/td,rd->tr/dot_general | solution.py:55
  30.6 0.7 all-gather.8.cloned.1.call-update
  31.5 0.5 broadcast.43
  32.0 0.7 reduce.11
  32.8 0.7 reduce.10
  33.8 1.9 all-gather.2
  36.1 15.8 %reduce-scatter.7.cloned.1.call-done = bf16[128,256]{1,0:T(8,128)(2,1)} async-done(((bf16[128,1024]{1,0:T(8,128)(2,1)}), bf16[128,256]{1,0:T(8,128)(2,1)}) %reduce-scatter.7.cloned.1.call-update) | async-done | bytes 65552 | tf_op jit(solution)/shard_map/reduce_scatter | solution.py:58
  51.9 6.2 %collective-permute-done = bf16[128,256]{1,0:T(8,128)(2,1)S(1)} collective-permute-done((bf16[128,256]{1,0:T(8,128)(2,1)}, bf16[128,256]{1,0:T(8,128)(2,1)S(1)}, u32[]{:S(2)}, u32[]{:S(2)}) %collective-permute-start) | collective-permute-done | bytes 65568 | tf_op jit(solution)/shard_map/ppermute | solution.py:64
  58.2 6.5 %collective-permute-done.1 = bf16[128,256]{1,0:T(8,128)(2,1)S(1)} collective-permute-done((bf16[128,256]{1,0:T(8,128)(2,1)S(1)}, bf16[128,256]{1,0:T(8,128)(2,1)S(1)}, u32[]{:S(2)}, u32[]{:S(2)}) %collective-permute-start.1) | collective-permute-done | bytes 65568 | tf_op jit(solution)/shard_map/ppermute | solution.py:64
  64.6 1.4 fusion.150
  66.0 4.7 %collective-permute-done.2 = bf16[128,256]{1,0:T(8,128)(2,1)S(1)} collective-permute-done((bf16[128,256]{1,0:T(8,128)(2,1)S(1)}, bf16[128,256]{1,0:T(8,128)(2,1)S(1)}, u32[]{:S(2)}, u32[]{:S(2)}) %collective-permute-start.2) | collective-permute-done | bytes 65568 | tf_op jit(solution)/shard_map/ppermute | solution.py:64
  70.8 5.2 %bitcast_dynamic-update-slice_fusion.3 = (bf16[2,128,2048]{2,1,0:T(8,128)(2,1)S(1)}, bf16[128,2048]{1,0:T(8,128)(2,1)}) fusion(bf16[2,128,2048]{2,1,0:T(8,128)(2,1)S(1)} %broadcast_in_dim.36, s32[]{:T(128)S(6)} %min.16, pred[]{:T(512)S(6)} %and.22, f32[16,8,16,128]{3,2,1,0:T(8,128)} %bitcast.281, bf16[1,2048,1024]{2,1,0:T(8,128)(2,1)} %all-gather.8.cloned.1.call-done, ...), kind=kOutput, calls=%fused_computation.123 | convolution fusion | flops 539754496 | bytes 6553609 | tf_op jit(solution)/shard_map/tr,dr->td/dot_general | solution.py:86
  76.0 1.3 collective-permute-start.3
  77.3 1.4 dynamic-slice_bitcast_fusion
  78.8 0.9 copy.71
  79.7 7.7 %collective-permute-done.3 = bf16[128,2048]{1,0:T(8,128)(2,1)} collective-permute-done((bf16[128,2048]{1,0:T(8,128)(2,1)}, bf16[128,2048]{1,0:T(8,128)(2,1)}, u32[]{:S(2)}, u32[]{:S(2)}) %collective-permute-start.3) | collective-permute-done | bytes 524320 | tf_op jit(solution)/shard_map/ppermute | solution.py:10
  87.4 4.6 %fusion.62 = bf16[128,1024]{1,0:T(8,128)(2,1)} fusion(bf16[1,1024,2048]{2,1,0:T(8,128)(2,1)} %all-gather.6.cloned.1.call-done, bf16[128,2048]{1,0:T(8,128)(2,1)} %collective-permute-done.3, bf16[2,128,2048]{2,1,0:T(8,128)(2,1)S(1)} %copy-done.1, s32[]{:T(128)S(6)} %min.17, pred[]{:T(512)S(6)} %eq.15), kind=kOutput, calls=%fused_computation.34 | convolution fusion | flops 537264128 | bytes 5505029 | tf_op jit(solution)/shard_map/td,rd->tr/dot_general | solution.py:55
  92.0 0.8 constant_dynamic-slice_fusion.2
  92.9 1.1 fusion.138
  94.4 18.5 %reduce-scatter.9.cloned.1.call-done = bf16[128,256]{1,0:T(8,128)(2,1)} async-done(((bf16[128,1024]{1,0:T(8,128)(2,1)}), bf16[128,256]{1,0:T(8,128)(2,1)}) %reduce-scatter.9.cloned.1.call-update) | async-done | bytes 65552 | tf_op jit(solution)/shard_map/reduce_scatter | solution.py:58
  113.1 6.1 %collective-permute-done.4 = bf16[128,256]{1,0:T(8,128)(2,1)S(1)} collective-permute-done((bf16[128,256]{1,0:T(8,128)(2,1)}, bf16[128,256]{1,0:T(8,128)(2,1)S(1)}, u32[]{:S(2)}, u32[]{:S(2)}) %collective-permute-start.4) | collective-permute-done | bytes 65568 | tf_op jit(solution)/shard_map/ppermute | solution.py:64
  119.2 6.5 %collective-permute-done.5 = bf16[128,256]{1,0:T(8,128)(2,1)S(1)} collective-permute-done((bf16[128,256]{1,0:T(8,128)(2,1)S(1)}, bf16[128,256]{1,0:T(8,128)(2,1)S(1)}, u32[]{:S(2)}, u32[]{:S(2)}) %collective-permute-start.5) | collective-permute-done | bytes 65568 | tf_op jit(solution)/shard_map/ppermute | solution.py:64
  126.1 5.7 %collective-permute-done.6 = bf16[128,256]{1,0:T(8,128)(2,1)S(1)} collective-permute-done((bf16[128,256]{1,0:T(8,128)(2,1)S(1)}, bf16[128,256]{1,0:T(8,128)(2,1)S(1)}, u32[]{:S(2)}, u32[]{:S(2)}) %collective-permute-start.6) | collective-permute-done | bytes 65568 | tf_op jit(solution)/shard_map/ppermute | solution.py:64
  131.8 5.0 %bitcast_dynamic-update-slice_fusion.2 = (bf16[2,128,2048]{2,1,0:T(8,128)(2,1)S(1)}, bf16[128,2048]{1,0:T(8,128)(2,1)}) fusion(bf16[2,128,2048]{2,1,0:T(8,128)(2,1)S(1)} %get-tuple-element.18, s32[]{:T(128)S(6)} %min.17, bf16[1,128,2048]{2,1,0:T(8,128)(2,1)} %constant_dynamic-slice_fusion.2, pred[]{:T(512)S(6)} %and.23, ...), kind=kOutput, calls=%fused_computation.120 | convolution fusion | flops 539754496 | bytes 7077897 | tf_op jit(solution)/shard_map/tr,dr->td/dot_general | solution.py:86
  136.8 1.3 collective-permute-start.7
  138.1 0.9 fusion.81
  139.0 0.9 copy.72
  140.1 1.9 fusion.83
  142.0 0.9 fusion.85
  142.9 5.2 %collective-permute-done.7 = bf16[128,2048]{1,0:T(8,128)(2,1)} collective-permute-done((bf16[128,2048]{1,0:T(8,128)(2,1)}, bf16[128,2048]{1,0:T(8,128)(2,1)}, u32[]{:S(2)}, u32[]{:S(2)}) %collective-permute-start.7) | collective-permute-done | bytes 524320 | tf_op jit(solution)/shard_map/ppermute | solution.py:10
  148.2 4.6 %fusion.65 = bf16[128,1024]{1,0:T(8,128)(2,1)} fusion(bf16[1,1024,2048]{2,1,0:T(8,128)(2,1)} %all-gather.6.cloned.1.call-done, bf16[128,2048]{1,0:T(8,128)(2,1)} %collective-permute-done.7, bf16[2,128,2048]{2,1,0:T(8,128)(2,1)S(1)} %copy-done.1, s32[]{:T(128)S(6)} %min.18, pred[]{:T(512)S(6)} %eq.15), kind=kOutput, calls=%fused_computation.35 | convolution fusion | flops 537264128 | bytes 5505029 | tf_op jit(solution)/shard_map/td,rd->tr/dot_general | solution.py:55
  152.8 0.8 constant_dynamic-slice_fusion.1
  153.6 1.1 fusion.139
  155.2 15.8 %reduce-scatter.11.cloned.1.call-done = bf16[128,256]{1,0:T(8,128)(2,1)} async-done(((bf16[128,1024]{1,0:T(8,128)(2,1)}), bf16[128,256]{1,0:T(8,128)(2,1)}) %reduce-scatter.11.cloned.1.call-update) | async-done | bytes 65552 | tf_op jit(solution)/shard_map/reduce_scatter | solution.py:58
  171.2 6.1 %collective-permute-done.8 = bf16[128,256]{1,0:T(8,128)(2,1)S(1)} collective-permute-done((bf16[128,256]{1,0:T(8,128)(2,1)}, bf16[128,256]{1,0:T(8,128)(2,1)S(1)}, u32[]{:S(2)}, u32[]{:S(2)}) %collective-permute-start.8) | collective-permute-done | bytes 65568 | tf_op jit(solution)/shard_map/ppermute | solution.py:64
  177.3 6.5 %collective-permute-done.9 = bf16[128,256]{1,0:T(8,128)(2,1)S(1)} collective-permute-done((bf16[128,256]{1,0:T(8,128)(2,1)S(1)}, bf16[128,256]{1,0:T(8,128)(2,1)S(1)}, u32[]{:S(2)}, u32[]{:S(2)}) %collective-permute-start.9) | collective-permute-done | bytes 65568 | tf_op jit(solution)/shard_map/ppermute | solution.py:64
  183.8 0.4 fusion.146
  184.2 5.6 %collective-permute-done.10 = bf16[128,256]{1,0:T(8,128)(2,1)S(1)} collective-permute-done((bf16[128,256]{1,0:T(8,128)(2,1)S(1)}, bf16[128,256]{1,0:T(8,128)(2,1)S(1)}, u32[]{:S(2)}, u32[]{:S(2)}) %collective-permute-start.10) | collective-permute-done | bytes 65568 | tf_op jit(solution)/shard_map/ppermute | solution.py:64
  189.8 5.0 %bitcast_dynamic-update-slice_fusion.1 = (bf16[2,128,2048]{2,1,0:T(8,128)(2,1)S(1)}, bf16[128,2048]{1,0:T(8,128)(2,1)}) fusion(bf16[2,128,2048]{2,1,0:T(8,128)(2,1)S(1)} %get-tuple-element.20, s32[]{:T(128)S(6)} %min.18, bf16[1,128,2048]{2,1,0:T(8,128)(2,1)} %constant_dynamic-slice_fusion.1, pred[]{:T(512)S(6)} %and.24, ...), kind=kOutput, calls=%fused_computation.117 | convolution fusion | flops 539754496 | bytes 7077897 | tf_op jit(solution)/shard_map/tr,dr->td/dot_general | solution.py:86
  194.9 1.3 collective-permute-start.11
  196.4 0.9 copy.74
  197.4 2.0 fusion.87
  199.6 6.6 %collective-permute-done.11 = bf16[128,2048]{1,0:T(8,128)(2,1)} collective-permute-done((bf16[128,2048]{1,0:T(8,128)(2,1)}, bf16[128,2048]{1,0:T(8,128)(2,1)}, u32[]{:S(2)}, u32[]{:S(2)}) %collective-permute-start.11) | collective-permute-done | bytes 524320 | tf_op jit(solution)/shard_map/ppermute | solution.py:10
  206.2 4.6 %fusion.68 = bf16[128,1024]{1,0:T(8,128)(2,1)} fusion(bf16[1,1024,2048]{2,1,0:T(8,128)(2,1)} %all-gather.6.cloned.1.call-done, bf16[128,2048]{1,0:T(8,128)(2,1)} %collective-permute-done.11, bf16[2,128,2048]{2,1,0:T(8,128)(2,1)S(1)} %copy-done.1, s32[]{:T(128)S(6)} %min.19, pred[]{:T(512)S(6)} %eq.15), kind=kOutput, calls=%fused_computation.36 | convolution fusion | flops 537264128 | bytes 5505029 | tf_op jit(solution)/shard_map/td,rd->tr/dot_general | solution.py:55
  210.9 1.1 fusion.140
  212.5 16.7 %reduce-scatter.13.cloned.1.call-done = bf16[128,256]{1,0:T(8,128)(2,1)} async-done(((bf16[128,1024]{1,0:T(8,128)(2,1)}), bf16[128,256]{1,0:T(8,128)(2,1)}) %reduce-scatter.13.cloned.1.call-update) | async-done | bytes 65552 | tf_op jit(solution)/shard_map/reduce_scatter | solution.py:58
  229.3 6.1 %collective-permute-done.12 = bf16[128,256]{1,0:T(8,128)(2,1)S(1)} collective-permute-done((bf16[128,256]{1,0:T(8,128)(2,1)}, bf16[128,256]{1,0:T(8,128)(2,1)S(1)}, u32[]{:S(2)}, u32[]{:S(2)}) %collective-permute-start.12) | collective-permute-done | bytes 65568 | tf_op jit(solution)/shard_map/ppermute | solution.py:64
  235.5 6.5 %collective-permute-done.13 = bf16[128,256]{1,0:T(8,128)(2,1)S(1)} collective-permute-done((bf16[128,256]{1,0:T(8,128)(2,1)S(1)}, bf16[128,256]{1,0:T(8,128)(2,1)S(1)}, u32[]{:S(2)}, u32[]{:S(2)}) %collective-permute-start.13) | collective-permute-done | bytes 65568 | tf_op jit(solution)/shard_map/ppermute | solution.py:64
  242.4 5.7 %collective-permute-done.14 = bf16[128,256]{1,0:T(8,128)(2,1)S(1)} collective-permute-done((bf16[128,256]{1,0:T(8,128)(2,1)S(1)}, bf16[128,256]{1,0:T(8,128)(2,1)S(1)}, u32[]{:S(2)}, u32[]{:S(2)}) %collective-permute-start.14) | collective-permute-done | bytes 65568 | tf_op jit(solution)/shard_map/ppermute | solution.py:64
  248.0 4.0 %bitcast_dynamic-update-slice_fusion = (bf16[2,128,2048]{2,1,0:T(8,128)(2,1)S(1)}, bf16[128,2048]{1,0:T(8,128)(2,1)S(1)}) fusion(bf16[2,128,2048]{2,1,0:T(8,128)(2,1)S(1)} %get-tuple-element.22, s32[]{:T(128)S(6)} %min.19, bf16[1,128,2048]{2,1,0:T(8,128)(2,1)S(1)} %constant_dynamic-slice_fusion, pred[]{:T(512)S(6)} %and.25, ...), kind=kOutput, calls=%fused_computation.114 | convolution fusion | flops 539754496 | bytes 7077897 | tf_op jit(solution)/shard_map/tr,dr->td/dot_general | solution.py:86
  252.1 1.6 collective-permute-start.15
  254.3 1.0 copy.135
  255.3 8.1 %collective-permute-done.15 = bf16[128,2048]{1,0:T(8,128)(2,1)S(1)} collective-permute-done((bf16[128,2048]{1,0:T(8,128)(2,1)S(1)}, bf16[128,2048]{1,0:T(8,128)(2,1)S(1)}, u32[]{:S(2)}, u32[]{:S(2)}) %collective-permute-start.15) | collective-permute-done | bytes 524320 | tf_op jit(solution)/shard_map/ppermute | solution.py:10
  263.6 2.3 fusion.71
  266.4 0.9 fusion.74
  267.3 17.0 %reduce-scatter.15.cloned.1.call-done = bf16[128,256]{1,0:T(8,128)(2,1)} async-done(((bf16[128,1024]{1,0:T(8,128)(2,1)}), bf16[128,256]{1,0:T(8,128)(2,1)}) %reduce-scatter.15.cloned.1.call-update) | async-done | bytes 65552 | tf_op jit(solution)/shard_map/reduce_scatter | solution.py:58
  284.4 6.3 %collective-permute-done.16 = bf16[128,256]{1,0:T(8,128)(2,1)S(1)} collective-permute-done((bf16[128,256]{1,0:T(8,128)(2,1)}, bf16[128,256]{1,0:T(8,128)(2,1)S(1)}, u32[]{:S(2)}, u32[]{:S(2)}) %collective-permute-start.16) | collective-permute-done | bytes 65568 | tf_op jit(solution)/shard_map/ppermute | solution.py:64
  290.6 0.4 fusion.142
  291.0 6.2 %collective-permute-done.17 = bf16[128,256]{1,0:T(8,128)(2,1)S(1)} collective-permute-done((bf16[128,256]{1,0:T(8,128)(2,1)S(1)}, bf16[128,256]{1,0:T(8,128)(2,1)S(1)}, u32[]{:S(2)}, u32[]{:S(2)}) %collective-permute-start.17) | collective-permute-done | bytes 65568 | tf_op jit(solution)/shard_map/ppermute | solution.py:64
  297.2 1.4 bitcast_convert_fusion
  298.6 4.7 %collective-permute-done.18 = bf16[128,256]{1,0:T(8,128)(2,1)S(1)} collective-permute-done((bf16[128,256]{1,0:T(8,128)(2,1)S(1)}, bf16[128,256]{1,0:T(8,128)(2,1)S(1)}, u32[]{:S(2)}, u32[]{:S(2)}) %collective-permute-start.18) | collective-permute-done | bytes 65568 | tf_op jit(solution)/shard_map/ppermute | solution.py:64
  303.2 4.8 %fusion.56 = bf16[1,2,128,2048]{3,2,1,0:T(8,128)(2,1)} fusion(bf16[1,2,128,2048]{3,2,1,0:T(8,128)(2,1)} %copy.135, s32[]{:T(128)S(6)} %min.20, bf16[1,2048,1024]{2,1,0:T(8,128)(2,1)} %all-gather.8.cloned.1.call-done, f32[16,8,16,128]{3,2,1,0:T(8,128)S(1)} %bitcast.282, bf16[2,128,2048]{2,1,0:T(8,128)(2,1)S(1)} %get-tuple-element.24, pred[]{:T(512)S(6)} %and.26, ...), kind=kOutput, calls=%fused_computation.32 | convolution fusion | flops 539754496 | bytes 6553609 | tf_op jit(solution)/shard_map/tr,dr->td/dot_general | solution.py:86
  (98 shorter events, 6.3 us)
Async XLA Ops:
  7.2 18.8 %all-gather.6.cloned.1.call-start = ((), (), s32[]{:S(2)}) async-start(), calls=%async_computation.12 | async-start | bytes 6291456 | tf_op jit(solution)/shard_map/all_gather | solution.py:24
  7.9 23.4 %copy-start.1 = (bf16[2,128,2048]{2,1,0:T(8,128)(2,1)S(1)}, bf16[2,128,2048]{2,1,0:T(8,128)(2,1)}, u32[]{:S(2)}) copy-start(bf16[2,128,2048]{2,1,0:T(8,128)(2,1)} %param.9) | copy-start | bytes 3145732
  7.9 43.9 %reduce-scatter.7.cloned.1.call-start = ((), (), s32[]{:S(2)}) async-start(), calls=%async_computation.6 | async-start | bytes 327680 | tf_op jit(solution)/shard_map/reduce_scatter | solution.py:58
  8.0 24.1 %copy-start.13 = (s32[1,8]{1,0:T(1,128)S(1)}, s32[1,8]{1,0:T(1,128)}, u32[]{:S(2)}) copy-start(s32[1,8]{1,0:T(1,128)} %param.14) | copy-start | bytes 100
  8.0 24.8 %copy-start.14 = (s32[1,8]{1,0:T(1,128)S(1)}, s32[1,8]{1,0:T(1,128)}, u32[]{:S(2)}) copy-start(s32[1,8]{1,0:T(1,128)} %param.15) | copy-start | bytes 100
  8.0 25.8 %copy-start.12 = (bf16[1,1,128,128]{3,2,1,0:T(8,128)(2,1)S(1)}, bf16[1,1,128,128]{3,2,1,0:T(8,128)(2,1)}, u32[]{:S(2)}) copy-start(bf16[1,1,128,128]{3,2,1,0:T(8,128)(2,1)} %param.13) | copy-start | bytes 98308
  30.5 35.5 %all-gather.8.cloned.1.call-start = ((), (), s32[]{:S(2)}) async-start(), calls=%async_computation.13 | async-start | bytes 6291456 | tf_op jit(solution)/shard_map/all_gather | solution.py:25
  31.3 81.6 %reduce-scatter.9.cloned.1.call-start = ((), (), s32[]{:S(2)}) async-start(), calls=%async_computation.7 | async-start | bytes 327680 | tf_op jit(solution)/shard_map/reduce_scatter | solution.py:58
  51.9 6.3 %collective-permute-start = (bf16[128,256]{1,0:T(8,128)(2,1)}, bf16[128,256]{1,0:T(8,128)(2,1)S(1)}, u32[]{:S(2)}, u32[]{:S(2)}) collective-permute-start(bf16[128,256]{1,0:T(8,128)(2,1)} %reduce-scatter.7.cloned.1.call-done), channel_id=1, source_target_pairs={{0,1},{1,2},{2,3},{3,0},{4,5},{5,6},{6,7},{7,4},{8,9},{9,10},{10,1... | collective-permute-start | bytes 196616 | tf_op jit(solution)/shard_map/ppermute | solution.py:64
  58.1 6.5 %collective-permute-start.1 = (bf16[128,256]{1,0:T(8,128)(2,1)S(1)}, bf16[128,256]{1,0:T(8,128)(2,1)S(1)}, u32[]{:S(2)}, u32[]{:S(2)}) collective-permute-start(bf16[128,256]{1,0:T(8,128)(2,1)S(1)} %collective-permute-done), channel_id=1, source_target_pairs={{0,1},{1,2},{2,3},{3,0},{4,5},{5,6},{6,7},{7,4},{8,9},{9,10},{10,1... | collective-permute-start | bytes 196616 | tf_op jit(solution)/shard_map/ppermute | solution.py:64
  64.6 6.1 %collective-permute-start.2 = (bf16[128,256]{1,0:T(8,128)(2,1)S(1)}, bf16[128,256]{1,0:T(8,128)(2,1)S(1)}, u32[]{:S(2)}, u32[]{:S(2)}) collective-permute-start(bf16[128,256]{1,0:T(8,128)(2,1)S(1)} %collective-permute-done.1), channel_id=1, source_target_pairs={{0,1},{1,2},{2,3},{3,0},{4,5},{5,6},{6,7},{7,4},{8,9},{9,10},{10,1... | collective-permute-start | bytes 196616 | tf_op jit(solution)/shard_map/ppermute | solution.py:64
  70.8 6.5 %copy-start.2 = (bf16[1,2,128,2048]{3,2,1,0:T(8,128)(2,1)S(1)}, bf16[1,2,128,2048]{3,2,1,0:T(8,128)(2,1)}, u32[]{:S(2)}) copy-start(bf16[1,2,128,2048]{3,2,1,0:T(8,128)(2,1)} %param.10) | copy-start | bytes 3145732
  76.0 11.4 %collective-permute-start.3 = (bf16[128,2048]{1,0:T(8,128)(2,1)}, bf16[128,2048]{1,0:T(8,128)(2,1)}, u32[]{:S(2)}, u32[]{:S(2)}) collective-permute-start(bf16[128,2048]{1,0:T(8,128)(2,1)} %get-tuple-element.19), channel_id=1, source_target_pairs={{8,0},{16,8},{24,16},{9,1},{17,9},{25,17},{10,2},{18,10},{26,18},{... | collective-permute-start | bytes 1572872 | tf_op jit(solution)/shard_map/ppermute | solution.py:10
  92.0 79.0 %reduce-scatter.11.cloned.1.call-start = ((), (), s32[]{:S(2)}) async-start(), calls=%async_computation.8 | async-start | bytes 327680 | tf_op jit(solution)/shard_map/reduce_scatter | solution.py:58
  112.9 6.3 %collective-permute-start.4 = (bf16[128,256]{1,0:T(8,128)(2,1)}, bf16[128,256]{1,0:T(8,128)(2,1)S(1)}, u32[]{:S(2)}, u32[]{:S(2)}) collective-permute-start(bf16[128,256]{1,0:T(8,128)(2,1)} %reduce-scatter.9.cloned.1.call-done), channel_id=1, source_target_pairs={{0,1},{1,2},{2,3},{3,0},{4,5},{5,6},{6,7},{7,4},{8,9},{9,10},{10,1... | collective-permute-start | bytes 196616 | tf_op jit(solution)/shard_map/ppermute | solution.py:64
  119.2 6.5 %collective-permute-start.5 = (bf16[128,256]{1,0:T(8,128)(2,1)S(1)}, bf16[128,256]{1,0:T(8,128)(2,1)S(1)}, u32[]{:S(2)}, u32[]{:S(2)}) collective-permute-start(bf16[128,256]{1,0:T(8,128)(2,1)S(1)} %collective-permute-done.4), channel_id=1, source_target_pairs={{0,1},{1,2},{2,3},{3,0},{4,5},{5,6},{6,7},{7,4},{8,9},{9,10},{10,1... | collective-permute-start | bytes 196616 | tf_op jit(solution)/shard_map/ppermute | solution.py:64
  125.7 6.1 %collective-permute-start.6 = (bf16[128,256]{1,0:T(8,128)(2,1)S(1)}, bf16[128,256]{1,0:T(8,128)(2,1)S(1)}, u32[]{:S(2)}, u32[]{:S(2)}) collective-permute-start(bf16[128,256]{1,0:T(8,128)(2,1)S(1)} %collective-permute-done.5), channel_id=1, source_target_pairs={{0,1},{1,2},{2,3},{3,0},{4,5},{5,6},{6,7},{7,4},{8,9},{9,10},{10,1... | collective-permute-start | bytes 196616 | tf_op jit(solution)/shard_map/ppermute | solution.py:64
  126.1 12.0 %copy-start.7 = (bf16[16,8,16,128]{3,2,1,0:T(8,128)(2,1)S(1)}, bf16[16,8,16,128]{3,2,1,0:T(8,128)(2,1)}, u32[]{:S(2)}) copy-start(bf16[16,8,16,128]{3,2,1,0:T(8,128)(2,1)} %copy.71) | copy-start | bytes 1572868
  131.8 7.2 %copy-start.6 = (bf16[16,8,16,128]{3,1,2,0:T(8,128)(2,1)S(1)}, bf16[16,8,16,128]{3,1,2,0:T(8,128)(2,1)}, u32[]{:S(2)}) copy-start(bf16[16,8,16,128]{3,1,2,0:T(8,128)(2,1)} %get-tuple-element.15) | copy-start | bytes 1572868
  131.8 8.2 %copy-start.5 = (bf16[16,8,16,128]{3,1,2,0:T(8,128)(2,1)S(1)}, bf16[16,8,16,128]{3,1,2,0:T(8,128)(2,1)}, u32[]{:S(2)}) copy-start(bf16[16,8,16,128]{3,1,2,0:T(8,128)(2,1)} %get-tuple-element.14) | copy-start | bytes 1572868
  136.8 11.4 %collective-permute-start.7 = (bf16[128,2048]{1,0:T(8,128)(2,1)}, bf16[128,2048]{1,0:T(8,128)(2,1)}, u32[]{:S(2)}, u32[]{:S(2)}) collective-permute-start(bf16[128,2048]{1,0:T(8,128)(2,1)} %get-tuple-element.21), channel_id=1, source_target_pairs={{8,0},{16,8},{24,16},{9,1},{17,9},{25,17},{10,2},{18,10},{26,18},{... | collective-permute-start | bytes 1572872 | tf_op jit(solution)/shard_map/ppermute | solution.py:10
  152.8 76.4 %reduce-scatter.13.cloned.1.call-start = ((), (), s32[]{:S(2)}) async-start(), calls=%async_computation.9 | async-start | bytes 327680 | tf_op jit(solution)/shard_map/reduce_scatter | solution.py:58
  171.0 6.3 %collective-permute-start.8 = (bf16[128,256]{1,0:T(8,128)(2,1)}, bf16[128,256]{1,0:T(8,128)(2,1)S(1)}, u32[]{:S(2)}, u32[]{:S(2)}) collective-permute-start(bf16[128,256]{1,0:T(8,128)(2,1)} %reduce-scatter.11.cloned.1.call-done), channel_id=1, source_target_pairs={{0,1},{1,2},{2,3},{3,0},{4,5},{5,6},{6,7},{7,4},{8,9},{9,10},{10,1... | collective-permute-start | bytes 196616 | tf_op jit(solution)/shard_map/ppermute | solution.py:64
  177.3 6.5 %collective-permute-start.9 = (bf16[128,256]{1,0:T(8,128)(2,1)S(1)}, bf16[128,256]{1,0:T(8,128)(2,1)S(1)}, u32[]{:S(2)}, u32[]{:S(2)}) collective-permute-start(bf16[128,256]{1,0:T(8,128)(2,1)S(1)} %collective-permute-done.8), channel_id=1, source_target_pairs={{0,1},{1,2},{2,3},{3,0},{4,5},{5,6},{6,7},{7,4},{8,9},{9,10},{10,1... | collective-permute-start | bytes 196616 | tf_op jit(solution)/shard_map/ppermute | solution.py:64
  183.8 6.1 %collective-permute-start.10 = (bf16[128,256]{1,0:T(8,128)(2,1)S(1)}, bf16[128,256]{1,0:T(8,128)(2,1)S(1)}, u32[]{:S(2)}, u32[]{:S(2)}) collective-permute-start(bf16[128,256]{1,0:T(8,128)(2,1)S(1)} %collective-permute-done.9), channel_id=1, source_target_pairs={{0,1},{1,2},{2,3},{3,0},{4,5},{5,6},{6,7},{7,4},{8,9},{9,10},{10,1... | collective-permute-start | bytes 196616 | tf_op jit(solution)/shard_map/ppermute | solution.py:64
  184.2 12.0 %copy-start.10 = (bf16[128,2,128]{2,1,0:T(2,128)(2,1)S(1)}, bf16[128,2,128]{2,1,0:T(2,128)(2,1)}, u32[]{:S(2)}) copy-start(bf16[128,2,128]{2,1,0:T(2,128)(2,1)} %fusion.81) | copy-start | bytes 196612
  189.8 6.5 %copy-start.4 = (bf16[16,8,16,128]{3,1,2,0:T(8,128)(2,1)S(1)}, bf16[16,8,16,128]{3,1,2,0:T(8,128)(2,1)}, u32[]{:S(2)}) copy-start(bf16[16,8,16,128]{3,1,2,0:T(8,128)(2,1)} %get-tuple-element.17) | copy-start | bytes 1572868
  189.8 7.4 %copy-start.3 = (bf16[16,8,16,128]{3,1,2,0:T(8,128)(2,1)S(1)}, bf16[16,8,16,128]{3,1,2,0:T(8,128)(2,1)}, u32[]{:S(2)}) copy-start(bf16[16,8,16,128]{3,1,2,0:T(8,128)(2,1)} %get-tuple-element.13) | copy-start | bytes 1572868
  194.9 11.4 %collective-permute-start.11 = (bf16[128,2048]{1,0:T(8,128)(2,1)}, bf16[128,2048]{1,0:T(8,128)(2,1)}, u32[]{:S(2)}, u32[]{:S(2)}) collective-permute-start(bf16[128,2048]{1,0:T(8,128)(2,1)} %get-tuple-element.23), channel_id=1, source_target_pairs={{8,0},{16,8},{24,16},{9,1},{17,9},{25,17},{10,2},{18,10},{26,18},{... | collective-permute-start | bytes 1572872 | tf_op jit(solution)/shard_map/ppermute | solution.py:10
  210.8 73.5 %reduce-scatter.15.cloned.1.call-start = ((), (), s32[]{:S(2)}) async-start(), calls=%async_computation.10 | async-start | bytes 327680 | tf_op jit(solution)/shard_map/reduce_scatter | solution.py:58
  229.2 6.3 %collective-permute-start.12 = (bf16[128,256]{1,0:T(8,128)(2,1)}, bf16[128,256]{1,0:T(8,128)(2,1)S(1)}, u32[]{:S(2)}, u32[]{:S(2)}) collective-permute-start(bf16[128,256]{1,0:T(8,128)(2,1)} %reduce-scatter.13.cloned.1.call-done), channel_id=1, source_target_pairs={{0,1},{1,2},{2,3},{3,0},{4,5},{5,6},{6,7},{7,4},{8,9},{9,10},{10,1... | collective-permute-start | bytes 196616 | tf_op jit(solution)/shard_map/ppermute | solution.py:64
  235.4 6.5 %collective-permute-start.13 = (bf16[128,256]{1,0:T(8,128)(2,1)S(1)}, bf16[128,256]{1,0:T(8,128)(2,1)S(1)}, u32[]{:S(2)}, u32[]{:S(2)}) collective-permute-start(bf16[128,256]{1,0:T(8,128)(2,1)S(1)} %collective-permute-done.12), channel_id=1, source_target_pairs={{0,1},{1,2},{2,3},{3,0},{4,5},{5,6},{6,7},{7,4},{8,9},{9,10},{10,1... | collective-permute-start | bytes 196616 | tf_op jit(solution)/shard_map/ppermute | solution.py:64
  242.0 6.1 %collective-permute-start.14 = (bf16[128,256]{1,0:T(8,128)(2,1)S(1)}, bf16[128,256]{1,0:T(8,128)(2,1)S(1)}, u32[]{:S(2)}, u32[]{:S(2)}) collective-permute-start(bf16[128,256]{1,0:T(8,128)(2,1)S(1)} %collective-permute-done.13), channel_id=1, source_target_pairs={{0,1},{1,2},{2,3},{3,0},{4,5},{5,6},{6,7},{7,4},{8,9},{9,10},{10,1... | collective-permute-start | bytes 196616 | tf_op jit(solution)/shard_map/ppermute | solution.py:64
  242.4 11.3 %copy-start.8 = (bf16[128,2,128]{2,1,0:T(2,128)(2,1)S(1)}, bf16[128,2,128]{2,1,0:T(2,128)(2,1)}, u32[]{:S(2)}) copy-start(bf16[128,2,128]{2,1,0:T(2,128)(2,1)} %fusion.83) | copy-start | bytes 196612
  248.0 5.9 %copy-start.9 = (bf16[128,2,128]{2,1,0:T(2,128)(2,1)S(1)}, bf16[128,2,128]{2,1,0:T(2,128)(2,1)}, u32[]{:S(2)}) copy-start(bf16[128,2,128]{2,1,0:T(2,128)(2,1)} %fusion.85) | copy-start | bytes 196612
  248.0 6.1 %copy-start.11 = (bf16[128,2,128]{2,1,0:T(2,128)(2,1)S(1)}, bf16[128,2,128]{2,1,0:T(2,128)(2,1)}, u32[]{:S(2)}) copy-start(bf16[128,2,128]{2,1,0:T(2,128)(2,1)} %fusion.87) | copy-start | bytes 196612
  252.1 11.5 %copy-start = (bf16[1,1024,2048]{2,1,0:T(8,128)(2,1)S(1)}, bf16[1,1024,2048]{2,1,0:T(8,128)(2,1)}, u32[]{:S(2)}) copy-start(bf16[1,1024,2048]{2,1,0:T(8,128)(2,1)} %all-gather.6.cloned.1.call-done) | copy-start | bytes 12582916
  252.1 11.3 %collective-permute-start.15 = (bf16[128,2048]{1,0:T(8,128)(2,1)S(1)}, bf16[128,2048]{1,0:T(8,128)(2,1)S(1)}, u32[]{:S(2)}, u32[]{:S(2)}) collective-permute-start(bf16[128,2048]{1,0:T(8,128)(2,1)S(1)} %get-tuple-element.25), channel_id=1, source_target_pairs={{8,0},{16,8},{24,16},{9,1},{17,9},{25,17},{10,2},{18,10},{26,18},{... | collective-permute-start | bytes 1572872 | tf_op jit(solution)/shard_map/ppermute | solution.py:10
  265.9 31.3 %reduce-scatter.17.cloned.1.call-start = ((), (), s32[]{:S(2)}) async-start(), calls=%async_computation.11 | async-start | bytes 98304 | tf_op jit(solution)/shard_map/reduce_scatter | solution.py:110
  284.3 6.3 %collective-permute-start.16 = (bf16[128,256]{1,0:T(8,128)(2,1)}, bf16[128,256]{1,0:T(8,128)(2,1)S(1)}, u32[]{:S(2)}, u32[]{:S(2)}) collective-permute-start(bf16[128,256]{1,0:T(8,128)(2,1)} %reduce-scatter.15.cloned.1.call-done), channel_id=1, source_target_pairs={{0,1},{1,2},{2,3},{3,0},{4,5},{5,6},{6,7},{7,4},{8,9},{9,10},{10,1... | collective-permute-start | bytes 196616 | tf_op jit(solution)/shard_map/ppermute | solution.py:64
  290.6 6.6 %collective-permute-start.17 = (bf16[128,256]{1,0:T(8,128)(2,1)S(1)}, bf16[128,256]{1,0:T(8,128)(2,1)S(1)}, u32[]{:S(2)}, u32[]{:S(2)}) collective-permute-start(bf16[128,256]{1,0:T(8,128)(2,1)S(1)} %collective-permute-done.16), channel_id=1, source_target_pairs={{0,1},{1,2},{2,3},{3,0},{4,5},{5,6},{6,7},{7,4},{8,9},{9,10},{10,1... | collective-permute-start | bytes 196616 | tf_op jit(solution)/shard_map/ppermute | solution.py:64
  297.2 6.1 %collective-permute-start.18 = (bf16[128,256]{1,0:T(8,128)(2,1)S(1)}, bf16[128,256]{1,0:T(8,128)(2,1)S(1)}, u32[]{:S(2)}, u32[]{:S(2)}) collective-permute-start(bf16[128,256]{1,0:T(8,128)(2,1)S(1)} %collective-permute-done.17), channel_id=1, source_target_pairs={{0,1},{1,2},{2,3},{3,0},{4,5},{5,6},{6,7},{7,4},{8,9},{9,10},{10,1... | collective-permute-start | bytes 196616 | tf_op jit(solution)/shard_map/ppermute | solution.py:64
Sparse Core Ops, SparseCore 0:
  9.5 16.3 all-gather.5
  30.7 21.1 reduce-scatter.6
  53.4 11.8 all-gather.7
  92.1 20.7 reduce-scatter.8
  152.9 18.0 reduce-scatter.10
  210.9 18.1 reduce-scatter.12
  266.0 18.2 reduce-scatter.14
  287.1 5.7 reduce-scatter.16
